TPU v7x, 32 devices: a whole 2x2x4 slice. The times are simulated.
32 devices in a mesh: row: 8 (over z, y), col: 4 (over x, core).
Axes of the slice: x: 2, y: 2, z: 4, core: 2. Of those that a mesh axis runs over, the one named last changes fastest.
Arguments:
- tile_u: bfloat16 [3, 8, 2, 4, 512, 128], P(None, 'row', None, 'col'), may hold values from -6 to 6
- tile_v: bfloat16 [3, 8, 2, 4, 512, 128], P(None, 'row', None, 'col'), may hold values from -6 to 6
- tile_ranks: int32 [3, 8, 2, 4], P(None, 'row', None, 'col'), may hold values from 16 to 128
- lower_inverse: bfloat16 [2, 512, 512], replicated, as said below
- upper_inverse: bfloat16 [2, 512, 512], replicated, as said below
- row_order: int32 [2, 512], replicated, may hold values from 0 to 511, each once within a row
- sketch: bfloat16 [512, 128], replicated, may hold values from -0.25 to 0.25
Outputs:
- new_u: bfloat16 [3, 8, 2, 4, 512, 128], P(None, 'row', None, 'col')
- new_v: bfloat16 [3, 8, 2, 4, 512, 128], P(None, 'row', None, 'col')
Inputs may be any that keep to these rules, and one draw needn't show every extreme that they name: Each row of row_order names every number of 0 to 511 once. Each lower_inverse[k] is lower triangular with a unit diagonal. Each upper_inverse[k] is upper triangular with a positive diagonal.
All inputs are finite; a program needn't handle non-finite values.
Results may differ from a plain program's by a relative error of at most 0.03.
Values may be sent and summed in bfloat16 or wider, within the bound.
A program may use at most 64 MiB of HBM per device.

v0:
```python
import jax
import jax.numpy as jnp
from jax import lax
from jax.sharding import PartitionSpec as P

PANELS = 2
HIGHEST = lax.Precision.HIGHEST


def from_root(array, axis, root):
    mine = lax.axis_index(axis) == root
    return lax.psum(jnp.where(mine, array, jnp.zeros_like(array)), axis)


def compress(tile_uf, tile_vf, left_u, coupling, top_v, keep_cols, sketch):
    rank_width = tile_uf.shape[-1]
    tile_size = tile_uf.shape[-2]
    product = jnp.einsum("...br,...rs->...bs", left_u, coupling, preferred_element_type=jnp.float32)
    update = (product * rank_width ** (-0.5)).astype(jnp.bfloat16)
    stacked_left = jnp.concatenate([tile_uf, -update], axis=-1)
    stacked_right = jnp.concatenate([tile_vf, top_v], axis=-1)
    probe_mat = jnp.einsum(
        "...bt,br->...tr", stacked_right, sketch, preferred_element_type=jnp.float32
    )
    left_wide = stacked_left.astype(jnp.float32)
    sample = (
        jnp.einsum("...bt,...tr->...br", left_wide, probe_mat, precision=HIGHEST)
        * keep_cols[..., None, :]
    )
    gram_matrix = jnp.einsum("...br,...bs->...rs", sample, sample, precision=HIGHEST)
    gram_matrix = gram_matrix + (1.0 - keep_cols)[..., :, None] * jnp.eye(
        rank_width, dtype=jnp.float32
    )
    factor = jnp.linalg.cholesky(gram_matrix)
    solved = lax.linalg.triangular_solve(
        factor, jnp.swapaxes(sample, -1, -2), left_side=True, lower=True
    )
    new_basis = jnp.swapaxes(solved, -1, -2)
    weights_q = jnp.einsum("...bt,...br->...tr", left_wide, new_basis, precision=HIGHEST)
    fresh_v = jnp.einsum(
        "...bt,...tr->...br", stacked_right.astype(jnp.float32), weights_q, precision=HIGHEST
    )
    return (
        (new_basis * tile_size**0.5).astype(jnp.bfloat16),
        (fresh_v * tile_size ** (-0.5)).astype(jnp.bfloat16),
    )


def on_device(tile_u, tile_v, tile_ranks, lower_inverse, upper_inverse, row_order, sketch):
    row_tiles, col_tiles = (tile_u.shape[0], tile_u.shape[2])
    tile_size, rank_width = (tile_u.shape[4], tile_u.shape[5])
    shape_four = (row_tiles, col_tiles, tile_size, rank_width)
    tile_rank = tile_ranks.reshape(row_tiles, col_tiles)
    keep_flags_mask = jnp.arange(rank_width, dtype=jnp.int32)[None, None, :] < tile_rank[:, :, None]
    keep_cols = keep_flags_mask.astype(jnp.float32)
    keep_half = keep_flags_mask.astype(jnp.bfloat16)[:, :, None, :]
    factor_left_bases = tile_u.reshape(shape_four) * keep_half
    factors_v = tile_v.reshape(shape_four) * keep_half
    row_place = lax.axis_index("row")
    col_place = lax.axis_index("col")
    global_rows = jnp.arange(row_tiles, dtype=jnp.int32) * lax.axis_size("row") + row_place
    global_cols = jnp.arange(col_tiles, dtype=jnp.int32) * lax.axis_size("col") + col_place

    def prepare(panel, factor_left_bases, factors_v):
        permuted = jnp.take(factor_left_bases[0], row_order[panel], axis=1)
        turned_u = jnp.einsum(
            "ab,mbr->mar", lower_inverse[panel], permuted, preferred_element_type=jnp.float32
        ).astype(jnp.bfloat16)
        top_u = jnp.where((global_cols > panel)[:, None, None], turned_u, factor_left_bases[0])
        transposed_right_basis = jnp.einsum(
            "ba,lbr->lar", upper_inverse[panel], factors_v[:, 0], preferred_element_type=jnp.float32
        )
        transposed_right_basis = (transposed_right_basis * tile_size**0.5).astype(jnp.bfloat16)
        left_right_basis = jnp.where(
            (global_rows > panel)[:, None, None], transposed_right_basis, factors_v[:, 0]
        )
        factor_left_bases = factor_left_bases.at[0].set(
            jnp.where(row_place == panel, top_u, factor_left_bases[0])
        )
        factors_v = factors_v.at[:, 0].set(
            jnp.where(col_place == panel, left_right_basis, factors_v[:, 0])
        )
        panel_upper_left_basis, panel_top_v = (
            from_root(top_u, "row", panel),
            from_root(factors_v[0], "row", panel),
        )
        panel_left_u, panel_left_right_basis = (
            from_root(factor_left_bases[:, 0], "col", panel),
            from_root(left_right_basis, "col", panel),
        )
        coupling = jnp.einsum(
            "nxu,ixp->niup",
            panel_left_right_basis,
            panel_upper_left_basis,
            preferred_element_type=jnp.float32,
        )
        coupling = (coupling * tile_size ** (-0.5)).astype(jnp.bfloat16)
        return (factor_left_bases, factors_v, panel_left_u, coupling, panel_top_v)

    def refresh(
        panel, block_u, block_v, left_u, coupling, top_v, keep_block, rows_block, cols_block
    ):
        left_full = jnp.broadcast_to(left_u[:, None], block_u.shape)
        top_full = jnp.broadcast_to(top_v[None, :], block_v.shape)
        fresh_u, fresh_v = compress(
            block_u, block_v, left_full, coupling, top_full, keep_block, sketch
        )
        chosen = ((rows_block > panel)[:, None] & (cols_block > panel)[None, :])[:, :, None, None]
        return (jnp.where(chosen, fresh_u, block_u), jnp.where(chosen, fresh_v, block_v))

    prepared = prepare(0, factor_left_bases, factors_v)
    for panel in range(PANELS):
        factor_left_bases, factors_v, left_u, coupling, top_v = prepared
        if panel + 1 < PANELS:
            head_u, head_v = refresh(
                panel,
                factor_left_bases[:1],
                factors_v[:1],
                left_u[:1],
                coupling[:1],
                top_v,
                keep_cols[:1],
                global_rows[:1],
                global_cols,
            )
            lateral_left_basis, side_v = refresh(
                panel,
                factor_left_bases[1:, :1],
                factors_v[1:, :1],
                left_u[1:],
                coupling[1:, :1],
                top_v[:1],
                keep_cols[1:, :1],
                global_rows[1:],
                global_cols[:1],
            )
            factor_left_bases = (
                factor_left_bases.at[:1].set(head_u).at[1:, :1].set(lateral_left_basis)
            )
            factors_v = factors_v.at[:1].set(head_v).at[1:, :1].set(side_v)
            prepared = prepare(panel + 1, factor_left_bases, factors_v)
            factor_left_bases, factors_v = (prepared[0], prepared[1])
            inner_u, inner_v = refresh(
                panel,
                factor_left_bases[1:, 1:],
                factors_v[1:, 1:],
                left_u[1:],
                coupling[1:, 1:],
                top_v[1:],
                keep_cols[1:, 1:],
                global_rows[1:],
                global_cols[1:],
            )
            factor_left_bases = factor_left_bases.at[1:, 1:].set(inner_u)
            factors_v = factors_v.at[1:, 1:].set(inner_v)
            prepared = (factor_left_bases, factors_v) + tuple(prepared[2:])
        else:
            factor_left_bases, factors_v = refresh(
                panel,
                factor_left_bases,
                factors_v,
                left_u,
                coupling,
                top_v,
                keep_cols,
                global_rows,
                global_cols,
            )
    return (factor_left_bases.reshape(tile_u.shape), factors_v.reshape(tile_v.shape))


def solution(mesh):
    in_specs = (
        P(None, "row", None, "col", None, None),
        P(None, "row", None, "col", None, None),
        P(None, "row", None, "col"),
        P(),
        P(),
        P(),
        P(),
    )
    out_specs = (P(None, "row", None, "col", None, None), P(None, "row", None, "col", None, None))
    return jax.shard_map(
        on_device, mesh=mesh, in_specs=in_specs, out_specs=out_specs, check_vma=False
    )
```

profile of v0, /device:TPU:0, one launch (start us, length us, event | category | flops | bytes accessed | tf_op | source)
XLA Modules:
  0.0 551.3 jit_solution(12464353481008873408)
XLA Ops:
  7.2 1.5 copy.185
  8.8 0.7 fusion.117
  11.5 2.1 gather_fusion
  13.6 1.8 fusion.90
  15.4 2.2 broadcast_select_fusion.6
  17.6 0.8 fusion.65
  18.4 1.1 broadcast_select_fusion.4
  19.7 0.8 select_bitcast_fusion.1
  20.7 0.7 slice_bitcast_fusion.5
  21.5 0.7 slice_bitcast_fusion.7
  23.4 0.7 broadcast_subtract_fusion
  24.8 0.7 fusion.136
  26.7 0.7 compare_and_fusion.2
  28.5 0.7 slice_bitcast_fusion.8
  29.3 28.2 %all-reduce.15.cloned.1.call-done = (bf16[3,512,128]{1,2,0:T(8,128)(2,1)}, bf16[3,512,128]{1,2,0:T(8,128)(2,1)}) async-done(((bf16[3,512,128]{1,2,0:T(8,128)(2,1)}, bf16[3,512,128]{1,2,0:T(8,128)(2,1)}), (bf16[3,512,128]{1,2,0:T(8,128)(2,1)}, bf16[3,512,128]{1,2,0:T(8,128)(2,1)})) %all-reduce.15.cloned.1.call-update) | async-done | bytes 786448 | tf_op jit(solution)/shard_map/psum | solution.py:12
  57.5 1.0 slice_bitcast_fusion.11
  58.6 75.1 %all-reduce.11.cloned.1.call-done = (bf16[2,512,128]{1,2,0:T(8,128)(2,1)}, bf16[2,512,128]{1,2,0:T(8,128)(2,1)}) async-done(((bf16[2,512,128]{1,2,0:T(8,128)(2,1)}, bf16[2,512,128]{1,2,0:T(8,128)(2,1)}), (bf16[2,512,128]{1,2,0:T(8,128)(2,1)}, bf16[2,512,128]{1,2,0:T(8,128)(2,1)})) %all-reduce.11.cloned.1.call-update) | async-done | bytes 524304 | tf_op jit(solution)/shard_map/psum | solution.py:12
  133.7 1.5 fusion.34
  135.2 1.9 fusion.21
  137.6 0.7 slice_bitcast_fusion.9
  138.6 0.7 convolution_multiply_fusion.11
  139.3 1.0 fusion.35
  140.5 23.6 %custom-call.20 = f32[1,2,128,128]{3,2,1,0:T(8,128)S(1)} custom-call(f32[1,2,128,128]{3,2,1,0:T(8,128)S(1)} %copy.193), custom_call_target="Cholesky" | custom-call | tf_op jit(solution)/shard_map/jit(cholesky)/cholesky | solution.py:34
  164.4 20.3 %custom-call.21 = f32[1,2,1,128,128]{3,4,2,1,0:T(8,128)} custom-call(f32[1,2,1,128,128]{4,3,2,1,0:T(8,128)S(1)} %select_bitcast_fusion.3), custom_call_target="InvertDiagBlocksLowerTriangular" | custom-call | tf_op jit(solution)/shard_map/triangular_solve | solution.py:35
  184.7 0.9 broadcast_in_dim.170
  185.7 1.3 fusion.62
  187.0 1.7 convolution_multiply_fusion.10
  188.7 2.5 convolution_add_fusion.1
  191.2 1.6 copy.201
  192.9 1.6 fusion.98
  194.5 24.9 %custom-call.26 = f32[2,1,128,128]{3,2,1,0:T(8,128)} custom-call(f32[2,1,128,128]{3,2,1,0:T(8,128)} %fusion.98), custom_call_target="Cholesky" | custom-call | tf_op jit(solution)/shard_map/jit(cholesky)/cholesky | solution.py:34
  219.4 0.9 fusion.105
  220.5 1.6 fusion.108
  222.1 21.3 %custom-call.27 = f32[2,1,1,128,128]{3,4,2,1,0:T(8,128)} custom-call(f32[2,1,1,128,128]{4,3,2,1,0:T(8,128)} %fusion.108), custom_call_target="InvertDiagBlocksLowerTriangular" | custom-call | tf_op jit(solution)/shard_map/triangular_solve/custom-call.4 | solution.py:35
  243.4 2.4 fusion.78
  245.8 1.5 fusion.81
  247.5 2.1 gather_fusion.1
  249.6 1.8 fusion.91
  251.4 2.1 broadcast_select_fusion.5
  253.7 0.8 fusion.64
  257.0 0.7 copy-done.60
  257.7 1.2 bitcast_dynamic-update-slice_fusion
  259.7 0.7 convolution_multiply_fusion.7
  260.4 1.0 convolution_add_fusion
  261.5 0.7 fusion.96
  262.2 24.3 %custom-call.28 = f32[2,1,128,128]{3,2,1,0:T(8,128)S(1)} custom-call(f32[2,1,128,128]{3,2,1,0:T(8,128)} %fusion.96), custom_call_target="Cholesky" | custom-call | tf_op jit(solution)/shard_map/jit(cholesky)/cholesky | solution.py:34
  286.6 0.8 broadcast_select_fusion.2
  287.6 20.1 %custom-call.29 = f32[2,1,1,128,128]{3,4,2,1,0:T(8,128)S(1)} custom-call(f32[2,1,1,128,128]{4,3,2,1,0:T(8,128)S(1)} %fusion.103), custom_call_target="InvertDiagBlocksLowerTriangular" | custom-call | tf_op jit(solution)/shard_map/triangular_solve/custom-call.4 | solution.py:35
  307.7 0.7 fusion.85
  308.4 1.4 fusion.84
  310.9 11.1 %all-reduce.13.cloned.1.call-done = (bf16[3,512,128]{1,2,0:T(8,128)(2,1)}, bf16[3,512,128]{1,2,0:T(8,128)(2,1)}) async-done(((bf16[3,512,128]{1,2,0:T(8,128)(2,1)}, bf16[3,512,128]{1,2,0:T(8,128)(2,1)}), (bf16[3,512,128]{1,2,0:T(8,128)(2,1)}, bf16[3,512,128]{1,2,0:T(8,128)(2,1)})) %all-reduce.13.cloned.1.call-update) | async-done | bytes 786448 | tf_op jit(solution)/shard_map/psum | solution.py:12
  322.0 1.2 copy.225
  323.2 74.9 %all-reduce.9.cloned.1.call-done = (bf16[2,512,128]{1,2,0:T(8,128)(2,1)}, bf16[2,512,128]{1,2,0:T(8,128)(2,1)}) async-done(((bf16[2,512,128]{1,2,0:T(8,128)(2,1)}, bf16[2,512,128]{1,2,0:T(8,128)(2,1)}), (bf16[2,512,128]{1,2,0:T(8,128)(2,1)}, bf16[2,512,128]{1,2,0:T(8,128)(2,1)})) %all-reduce.9.cloned.1.call-update) | async-done | bytes 524304 | tf_op jit(solution)/shard_map/psum | solution.py:12
  398.1 1.0 broadcast_in_dim.178
  401.2 1.6 convolution_multiply_fusion
  402.8 2.6 fusion.137
  405.7 1.0 fusion.69
  406.6 71.3 %custom-call.22 = f32[3,2,128,128]{3,2,1,0:T(8,128)S(1)} custom-call(f32[3,2,128,128]{3,2,1,0:T(8,128)} %fusion.69), custom_call_target="Cholesky" | custom-call | tf_op jit(solution)/shard_map/jit(cholesky)/cholesky | solution.py:34
  478.3 59.0 %custom-call.23 = f32[3,2,1,128,128]{3,4,2,1,0:T(8,128)S(1)} custom-call(f32[3,2,1,128,128]{4,3,2,1,0:T(8,128)S(1)} %select_bitcast_fusion), custom_call_target="InvertDiagBlocksLowerTriangular" | custom-call | tf_op jit(solution)/shard_map/triangular_solve | solution.py:35
  537.3 1.5 fusion.66
  538.8 1.4 fusion.41
  540.7 1.2 copy.238
  542.3 1.1 fusion.5
  543.4 1.2 copy.239
  (199 shorter events, 15.2 us)
Async XLA Ops:
  7.2 131.1 %copy-start = (bf16[512,128]{1,0:T(8,128)(2,1)S(1)}, bf16[512,128]{1,0:T(8,128)(2,1)}, u32[]{:S(2)}) copy-start(bf16[512,128]{1,0:T(8,128)(2,1)} %param.38) | copy-start | bytes 393220
  7.2 1.6 copy-start.55
  7.2 2.3 copy-start.16
  7.2 50.3 %all-reduce.15.cloned.1.call-start = ((), (), s32[]{:S(2)}) async-start(), calls=%async_computation.3 | async-start | bytes 1572864 | tf_op jit(solution)/shard_map/psum | solution.py:12
  8.8 1.1 copy-start.44
  15.3 3.1 copy-start.59
  19.5 1.9 copy-start.11
  19.6 114.2 %all-reduce.11.cloned.1.call-start = ((), (), s32[]{:S(2)}) async-start(), calls=%async_computation.1 | async-start | bytes 1048576 | tf_op jit(solution)/shard_map/psum | solution.py:12
  19.7 1.7 copy-start.1
  20.5 1.7 copy-start.42
  20.5 3.0 copy-start.45
  20.5 301.5 %all-reduce.13.cloned.1.call-start = ((), (), s32[]{:S(2)}) async-start(), calls=%async_computation.2 | async-start | bytes 1572864 | tf_op jit(solution)/shard_map/psum | solution.py:12
  21.4 115.7 %copy-start.19 = (f32[128,128]{1,0:T(8,128)}, f32[128,128]{1,0:T(8,128)S(1)}, u32[]{:S(2)}) copy-start(f32[128,128]{1,0:T(8,128)S(1)} %fusion.116) | copy-start | bytes 196612
  21.4 142.7 %copy-start.22 = (pred[128,128]{1,0:T(8,128)(4,1)}, pred[128,128]{1,0:T(8,128)(4,1)S(1)}, u32[]{:S(2)}) copy-start(pred[128,128]{1,0:T(8,128)(4,1)S(1)} %iota_compare_fusion.1) | copy-start | bytes 49156
  22.8 114.5 %copy-start.61 = (pred[3]{0:T(512)(128)(4,1)}, pred[3]{0:T(512)(128)(4,1)S(1)}, u32[]{:S(2)}) copy-start(pred[3]{0:T(512)(128)(4,1)S(1)} %broadcast_compare_fusion.3) | copy-start | bytes 13
  24.7 112.6 %copy-start.56 = (pred[2]{0:T(512)(128)(4,1)}, pred[2]{0:T(512)(128)(4,1)S(1)}, u32[]{:S(2)}) copy-start(pred[2]{0:T(512)(128)(4,1)S(1)} %get-tuple-element.176) | copy-start | bytes 10
  24.8 160.9 %copy-start.14 = (f32[128,128]{0,1:T(8,128)}, f32[128,128]{0,1:T(8,128)S(1)}, u32[]{:S(2)}) copy-start(f32[128,128]{0,1:T(8,128)S(1)} %copy.190) | copy-start | bytes 196612
  57.5 79.6 %copy-start.13 = (bf16[3,512,128]{1,2,0:T(8,128)(2,1)S(1)}, bf16[3,512,128]{1,2,0:T(8,128)(2,1)}, u32[]{:S(2)}) copy-start(bf16[3,512,128]{1,2,0:T(8,128)(2,1)} %get-tuple-element.139) | copy-start | bytes 1179652
  133.7 3.8 copy-start.32
  133.7 4.5 copy-start.35
  185.6 1.3 copy-start.28
  243.4 2.4 copy-start.40
  243.4 2.4 copy-start.51
  245.8 1.7 copy-start.46
  245.8 3.8 copy-start.54
  247.3 4.1 copy-start.57
  251.4 3.1 copy-start.10
  253.6 1.6 copy-start.2
  253.6 1.6 copy-start.33
  253.6 1.6 copy-start.36
  253.6 1.6 copy-start.53
  254.5 1.1 copy-start.5
  254.5 1.2 copy-start.6
  254.5 1.3 copy-start.9
  255.2 1.2 copy-start.12
  255.2 1.2 copy-start.29
  255.2 1.2 copy-start.34
  255.2 1.2 copy-start.52
  256.5 1.2 copy-start.60
  256.5 1.2 copy-start.62
  257.7 1.2 copy-start.21
  258.9 0.8 copy-start.49
  258.9 1.5 copy-start.15
  258.9 1.6 copy-start.48
  259.7 26.8 %copy-start.23 = (pred[128,128]{1,0:T(8,128)(4,1)S(1)}, pred[128,128]{1,0:T(8,128)(4,1)}, u32[]{:S(2)}) copy-start(pred[128,128]{1,0:T(8,128)(4,1)} %copy-done.22) | copy-start | bytes 49156
  259.7 26.9 %copy-start.26 = (bf16[3,512,128]{1,2,0:T(8,128)(2,1)S(1)}, bf16[3,512,128]{1,2,0:T(8,128)(2,1)}, u32[]{:S(2)}) copy-start(bf16[3,512,128]{1,2,0:T(8,128)(2,1)} %get-tuple-element.170) | copy-start | bytes 1179652
  287.4 110.7 %all-reduce.9.cloned.1.call-start = ((), (), s32[]{:S(2)}) async-start(), calls=%async_computation | async-start | bytes 1048576 | tf_op jit(solution)/shard_map/psum | solution.py:12
  308.4 2.1 copy-start.31
  308.4 2.1 copy-start.38
  308.4 2.1 copy-start.50
  310.9 88.8 %copy-start.7 = (bf16[3,2,512,128]{2,3,1,0:T(8,128)(2,1)}, bf16[3,2,512,128]{2,3,1,0:T(8,128)(2,1)S(1)}, u32[]{:S(2)}) copy-start(bf16[3,2,512,128]{2,3,1,0:T(8,128)(2,1)S(1)} %fusion.40) | copy-start | bytes 2359300
  399.1 0.9 copy-start.17
  399.1 1.3 copy-start.25
  399.1 1.3 copy-start.39
  400.1 1.1 copy-start.43
  401.2 1.6 copy-start.3
  402.8 2.9 copy-start.20
  402.8 2.9 copy-start.27
  402.8 2.9 copy-start.41
  405.5 72.5 %copy-start.24 = (pred[128,128]{1,0:T(8,128)(4,1)S(1)}, pred[128,128]{1,0:T(8,128)(4,1)}, u32[]{:S(2)}) copy-start(pred[128,128]{1,0:T(8,128)(4,1)} %copy-done.22) | copy-start | bytes 49156
  537.3 1.5 copy-start.4
  538.8 1.4 copy-start.58
  540.7 1.2 copy-start.8
  540.7 1.6 copy-start.18
  (3 other events, 2.2 us)
Sparse Core Ops, SparseCore 0:
  19.7 37.7 all-reduce.14
  61.0 72.7 all-reduce.10
  287.6 34.3 all-reduce.12
  325.3 72.7 all-reduce.8
where the time goes:
time: 557 us; the launch traced here: 551 us
  other arithmetic  285 us (51%)
  waiting for transfers between devices  189 us (34%)
  matrix products  37.8 us (7%)
  local copies, waits for them, and re-layouts  22.4 us (4%)
  between operations  16.4 us (3%)
    psum x4, waiting for transfers between devices, from_root(): return lax.psum(jnp.where(mine, array, jnp.zeros_like(array)), axis)  189 us
    another operation x13, other arithmetic, compress(): factor = jnp.linalg.cholesky(gram_matrix)  146 us
    another operation x9, other arithmetic, compress(): lax.linalg.triangular_solve(factor, jnp.swapaxes(sample, -1, -2), left_si...  123 us
  transfers between devices with their start and end apart: 4, of which 4 were waited for; matrix products, arithmetic and copies ran while one was open for 6% of the time, Pallas kernels for 0%

commit v1 on v0

--- a/solution.py
+++ b/solution.py
@@ -9,7 +9,7 @@
 
 def from_root(array, axis, root):
     mine = lax.axis_index(axis) == root
-    return lax.psum(jnp.where(mine, array, jnp.zeros_like(array)), axis)
+    return jnp.sum(lax.all_gather(jnp.where(mine, array, jnp.zeros_like(array)), axis), axis=0)
 
 
 def compress(tile_uf, tile_vf, left_u, coupling, top_v, keep_cols, sketch):

time: 557 us -> 577 us (1.036)
  other arithmetic: 285 us -> 296 us
  local copies, waits for them, and re-layouts: 22.4 us -> 29 us
  waiting for transfers between devices: 189 us -> 195 us
    all_gather x0 -> x8, waiting for transfers between devices: none -> 195 us  [from_root(): lax.all_gather(jnp.where(mine, array, jnp.zeros_like(array)), axis)]
    psum x4 -> x0, waiting for transfers between devices: 189 us -> none  [from_root(): return lax.psum(jnp.where(mine, array, jnp.zeros_like(array)), axis)]
    reduce_sum x0 -> x8, other arithmetic: none -> 14.9 us  [from_root(): jnp.sum(lax.all_gather(jnp.where(mine, array, jnp.zeros_like(array)), axi...]
    select_n x0 -> x8, local copies, waits for them, and re-layouts: none -> 7.24 us  [from_root(): jnp.where(mine, array, jnp.zeros_like(array))]
  transfers between devices with their start and end apart: 4 -> 8, of which waited for: 4 -> 6; matrix products, arithmetic and copies ran while one was open for 6% -> 16% of each run, Pallas kernels for 0% -> 0%
where the time goes in v1:
time: 577 us; the launch traced here: 570 us
  other arithmetic  296 us (51%)
  waiting for transfers between devices  195 us (34%)
  matrix products  32.6 us (6%)
  local copies, waits for them, and re-layouts  29 us (5%)
  between operations  17.1 us (3%)
    all_gather x8, waiting for transfers between devices, from_root(): lax.all_gather(jnp.where(mine, array, jnp.zeros_like(array)), axis)  195 us
    another operation x13, other arithmetic, compress(): factor = jnp.linalg.cholesky(gram_matrix)  146 us
    another operation x9, other arithmetic, compress(): lax.linalg.triangular_solve(factor, jnp.swapaxes(sample, -1, -2), left_si...  121 us
    reduce_sum x8, other arithmetic, from_root(): jnp.sum(lax.all_gather(jnp.where(mine, array, jnp.zeros_like(array)), axi...  14.9 us
  transfers between devices with their start and end apart: 8, of which 6 were waited for; matrix products, arithmetic and copies ran while one was open for 16% of the time, Pallas kernels for 0%

profile of v1, /device:TPU:0, one launch (start us, length us, event | category | flops | bytes accessed | tf_op | source)
XLA Modules:
  0.0 570.0 jit_solution(8653391741267884730)
XLA Ops:
  7.8 0.8 copy.335
  9.2 1.4 copy.334
  11.1 1.0 copy-done.50
  12.5 0.9 copy.345
  14.7 2.1 gather_fusion
  17.9 1.7 fusion.87
  19.6 1.4 broadcast_select_fusion.7
  21.1 0.9 copy.340
  22.2 0.9 copy.350
  23.2 0.9 copy.343
  32.8 3.2 all-gather.23.cloned.1.call-done
  36.0 1.7 reduce_sum.98
  37.7 20.1 %all-gather.19.cloned.1.call-done = bf16[12,1,512,128]{3,2,1,0:T(8,128)(2,1)} async-done(((bf16[3,1,512,128]{3,2,1,0:T(8,128)(2,1)}), bf16[12,1,512,128]{3,2,1,0:T(8,128)(2,1)}) %all-gather.19.cloned.1.call-update) | async-done | bytes 1572880 | tf_op jit(solution)/shard_map/all_gather | solution.py:12
  57.8 1.6 bitcast_reduce_fusion.1
  59.4 49.6 %all-gather.15.cloned.1.call-done = bf16[8,2,512,128]{3,2,1,0:T(8,128)(2,1)} async-done(((bf16[1,2,512,128]{3,2,1,0:T(8,128)(2,1)}), bf16[8,2,512,128]{3,2,1,0:T(8,128)(2,1)}) %all-gather.15.cloned.1.call-update) | async-done | bytes 2097168 | tf_op jit(solution)/shard_map/all_gather | solution.py:12
  109.0 2.0 reduce_sum.99
  111.0 0.9 copy.351
  112.5 46.1 %all-gather.21.cloned.1.call-done = bf16[16,512,128]{2,1,0:T(8,128)(2,1)} async-done(((bf16[2,512,128]{2,1,0:T(8,128)(2,1)}), bf16[16,512,128]{2,1,0:T(8,128)(2,1)}) %all-gather.21.cloned.1.call-update) | async-done | bytes 2097168 | tf_op jit(solution)/shard_map/all_gather | solution.py:12
  158.7 2.0 reduce_sum.97
  160.6 0.8 copy.362
  161.7 1.0 fusion.21
  163.0 1.4 fusion.63
  165.1 1.0 fusion.35
  166.2 0.8 copy.356
  166.9 0.9 fusion.105
  167.9 23.6 %custom-call.20 = f32[1,2,128,128]{3,2,1,0:T(8,128)S(1)} custom-call(f32[1,2,128,128]{3,2,1,0:T(8,128)S(1)} %copy.357), custom_call_target="Cholesky" | custom-call | tf_op jit(solution)/shard_map/jit(cholesky)/cholesky | solution.py:34
  191.6 0.8 select_reduce_fusion.1
  192.5 20.3 %custom-call.21 = f32[1,2,1,128,128]{3,4,2,1,0:T(8,128)} custom-call(f32[1,2,1,128,128]{4,3,2,1,0:T(8,128)S(1)} %select_bitcast_fusion.2), custom_call_target="InvertDiagBlocksLowerTriangular" | custom-call | tf_op jit(solution)/shard_map/triangular_solve | solution.py:35
  212.9 1.3 fusion.62
  214.2 1.7 convolution_multiply_fusion.10
  215.9 1.8 convolution_add_fusion.1
  218.5 1.6 fusion.93
  220.1 24.3 %custom-call.26 = f32[2,1,128,128]{3,2,1,0:T(8,128)S(1)} custom-call(f32[2,1,128,128]{3,2,1,0:T(8,128)} %fusion.93), custom_call_target="Cholesky" | custom-call | tf_op jit(solution)/shard_map/jit(cholesky)/cholesky | solution.py:34
  244.4 0.8 fusion.100
  246.0 20.7 %custom-call.27 = f32[2,1,1,128,128]{3,4,2,1,0:T(8,128)S(1)} custom-call(f32[2,1,1,128,128]{4,3,2,1,0:T(8,128)} %fusion.103), custom_call_target="InvertDiagBlocksLowerTriangular" | custom-call | tf_op jit(solution)/shard_map/triangular_solve/custom-call.4 | solution.py:35
  266.7 1.7 fusion.76
  272.7 1.0 copy.395
  274.0 2.1 gather_fusion.1
  276.1 1.8 fusion.88
  277.9 1.4 broadcast_select_fusion.5
  279.4 0.9 copy.390
  280.4 0.9 copy.393
  281.4 0.9 copy.401
  283.8 1.1 fusion.19
  285.6 1.4 convolution_multiply_fusion.7
  287.1 1.0 convolution_add_fusion
  288.2 23.9 %custom-call.28 = f32[2,1,128,128]{3,2,1,0:T(8,128)S(1)} custom-call(f32[2,1,128,128]{3,2,1,0:T(8,128)S(1)} %fusion.91), custom_call_target="Cholesky" | custom-call | tf_op jit(solution)/shard_map/jit(cholesky)/cholesky | solution.py:34
  312.3 19.8 %custom-call.29 = f32[2,1,1,128,128]{3,4,2,1,0:T(8,128)S(1)} custom-call(f32[2,1,1,128,128]{4,3,2,1,0:T(8,128)S(1)} %fusion.98), custom_call_target="InvertDiagBlocksLowerTriangular" | custom-call | tf_op jit(solution)/shard_map/triangular_solve/custom-call.4 | solution.py:35
  334.0 2.0 reduce_sum.102
  336.1 1.6 bitcast_reduce_fusion
  337.7 27.7 %all-gather.27.cloned.1.call-done = bf16[16,512,128]{2,1,0:T(8,128)(2,1)} async-done(((bf16[2,512,128]{2,1,0:T(8,128)(2,1)}), bf16[16,512,128]{2,1,0:T(8,128)(2,1)}) %all-gather.27.cloned.1.call-update) | async-done | bytes 2097168 | tf_op jit(solution)/shard_map/all_gather | solution.py:12
  365.4 2.0 reduce_sum.101
  367.3 47.8 %all-gather.17.cloned.1.call-done = bf16[8,2,512,128]{3,2,1,0:T(8,128)(2,1)} async-done(((bf16[1,2,512,128]{3,2,1,0:T(8,128)(2,1)}), bf16[8,2,512,128]{3,2,1,0:T(8,128)(2,1)}) %all-gather.17.cloned.1.call-update) | async-done | bytes 2097168 | tf_op jit(solution)/shard_map/all_gather | solution.py:12
  415.1 2.0 reduce_sum.103
  419.1 1.6 convolution_multiply_fusion
  420.7 2.6 fusion.132
  423.6 0.9 fusion.69
  424.5 71.3 %custom-call.22 = f32[3,2,128,128]{3,2,1,0:T(8,128)S(1)} custom-call(f32[3,2,128,128]{3,2,1,0:T(8,128)} %fusion.69), custom_call_target="Cholesky" | custom-call | tf_op jit(solution)/shard_map/jit(cholesky)/cholesky | solution.py:34
  496.2 59.0 %custom-call.23 = f32[3,2,1,128,128]{3,4,2,1,0:T(8,128)S(1)} custom-call(f32[3,2,1,128,128]{4,3,2,1,0:T(8,128)S(1)} %select_bitcast_fusion), custom_call_target="InvertDiagBlocksLowerTriangular" | custom-call | tf_op jit(solution)/shard_map/triangular_solve | solution.py:35
  555.2 1.5 fusion.66
  556.7 1.4 fusion.41
  559.5 1.1 fusion.5
  560.7 1.2 copy.412
  561.8 1.2 copy.411
  (209 shorter events, 28.5 us)
Async XLA Ops:
  7.2 155.8 %copy-start = (bf16[512,128]{1,0:T(8,128)(2,1)S(1)}, bf16[512,128]{1,0:T(8,128)(2,1)}, u32[]{:S(2)}) copy-start(bf16[512,128]{1,0:T(8,128)(2,1)} %param.38) | copy-start | bytes 393220
  7.2 3.4 copy-start.16
  7.2 28.8 %all-gather.23.cloned.1.call-start = ((), (), s32[]{:S(2)}) async-start(), calls=%async_computation.4 | async-start | bytes 1966080 | tf_op jit(solution)/shard_map/all_gather | solution.py:12
  8.5 2.3 copy-start.38
  10.9 1.2 copy-start.50
  12.5 9.6 %copy-start.11 = (bf16[3,512,128]{1,2,0:T(8,128)(2,1)}, bf16[3,512,128]{1,2,0:T(8,128)(2,1)S(1)}, u32[]{:S(2)}) copy-start(bf16[3,512,128]{1,2,0:T(8,128)(2,1)S(1)} %get-tuple-element.140) | copy-start | bytes 1179652
  13.4 0.7 copy-start.41
  13.5 44.3 %all-gather.19.cloned.1.call-start = ((), (), s32[]{:S(2)}) async-start(), calls=%async_computation.2 | async-start | bytes 1966080 | tf_op jit(solution)/shard_map/all_gather | solution.py:12
  22.1 87.0 %all-gather.15.cloned.1.call-start = ((), (), s32[]{:S(2)}) async-start(), calls=%async_computation | async-start | bytes 2359296 | tf_op jit(solution)/shard_map/all_gather | solution.py:12
  22.2 8.4 %copy-start.1 = (bf16[3,2,512,128]{2,3,0,1:T(8,128)(2,1)}, bf16[3,2,512,128]{2,3,0,1:T(8,128)(2,1)S(1)}, u32[]{:S(2)}) copy-start(bf16[3,2,512,128]{2,3,0,1:T(8,128)(2,1)S(1)} %bitcast_dynamic-update-slice_fusion.1) | copy-start | bytes 2359300
  23.1 6.4 %copy-start.36 = (f32[3,2,128]{2,1,0:T(2,128)S(1)}, f32[3,2,128]{2,1,0:T(2,128)}, u32[]{:S(2)}) copy-start(f32[3,2,128]{2,1,0:T(2,128)} %get-tuple-element.151) | copy-start | bytes 9220
  23.1 135.5 %all-gather.21.cloned.1.call-start = ((), (), s32[]{:S(2)}) async-start(), calls=%async_computation.3 | async-start | bytes 2359296 | tf_op jit(solution)/shard_map/all_gather | solution.py:12
  23.2 8.1 %copy-start.12 = (bf16[3,512,128]{1,2,0:T(8,128)(2,1)S(1)}, bf16[3,512,128]{1,2,0:T(8,128)(2,1)}, u32[]{:S(2)}) copy-start(bf16[3,512,128]{1,2,0:T(8,128)(2,1)} %copy-done.11) | copy-start | bytes 1179652
  24.1 309.9 %all-gather.29.cloned.1.call-start = ((), (), s32[]{:S(2)}) async-start(), calls=%async_computation.7 | async-start | bytes 1966080 | tf_op jit(solution)/shard_map/all_gather | solution.py:12
  26.9 10.8 %copy-start.20 = (f32[128,128]{1,0:T(8,128)}, f32[128,128]{1,0:T(8,128)S(1)}, u32[]{:S(2)}) copy-start(f32[128,128]{1,0:T(8,128)S(1)} %get-tuple-element.180) | copy-start | bytes 196612
  161.4 3.0 copy-start.43
  161.7 3.4 copy-start.19
  162.7 2.4 copy-start.14
  162.7 2.4 copy-start.42
  163.0 3.2 copy-start.5
  165.1 47.7 %copy-start.22 = (bf16[512,128]{0,1:T(8,128)(2,1)S(1)}, bf16[512,128]{0,1:T(8,128)(2,1)}, u32[]{:S(2)}) copy-start(bf16[512,128]{0,1:T(8,128)(2,1)} %copy.362) | copy-start | bytes 393220
  212.8 1.4 copy-start.26
  266.7 1.8 copy-start.6
  266.7 2.4 copy-start.2
  266.7 2.4 copy-start.31
  266.7 2.4 copy-start.32
  266.7 2.4 copy-start.48
  268.4 1.2 copy-start.46
  269.1 1.1 copy-start.7
  269.1 1.1 copy-start.8
  269.5 1.4 copy-start.13
  269.6 1.4 copy-start.27
  269.6 1.4 copy-start.30
  271.0 1.2 copy-start.51
  271.0 1.2 copy-start.52
  272.6 1.1 copy-start.40
  272.7 3.4 copy-start.47
  272.7 5.2 copy-start.53
  273.7 62.3 %all-gather.25.cloned.1.call-start = ((), (), s32[]{:S(2)}) async-start(), calls=%async_computation.5 | async-start | bytes 1966080 | tf_op jit(solution)/shard_map/all_gather | solution.py:12
  279.4 3.5 copy-start.39
  280.4 85.0 %all-gather.27.cloned.1.call-start = ((), (), s32[]{:S(2)}) async-start(), calls=%async_computation.6 | async-start | bytes 2359296 | tf_op jit(solution)/shard_map/all_gather | solution.py:12
  280.4 3.2 copy-start.23
  281.3 133.8 %all-gather.17.cloned.1.call-start = ((), (), s32[]{:S(2)}) async-start(), calls=%async_computation.1 | async-start | bytes 2359296 | tf_op jit(solution)/shard_map/all_gather | solution.py:12
  283.7 1.6 copy-start.33
  284.9 2.2 copy-start.15
  284.9 2.2 copy-start.44
  284.9 0.7 copy-start.28
  285.6 26.4 %copy-start.24 = (pred[128,128]{1,0:T(8,128)(4,1)S(1)}, pred[128,128]{1,0:T(8,128)(4,1)}, u32[]{:S(2)}) copy-start(pred[128,128]{1,0:T(8,128)(4,1)} %iota_compare_fusion.1) | copy-start | bytes 49156
  285.6 46.5 %copy-start.45 = (pred[2]{0:T(512)(128)(4,1)S(1)}, pred[2]{0:T(512)(128)(4,1)}, u32[]{:S(2)}) copy-start(pred[2]{0:T(512)(128)(4,1)} %get-tuple-element.155) | copy-start | bytes 10
  332.2 1.4 copy-start.29
  332.2 1.4 copy-start.34
  334.0 84.1 %copy-start.9 = (bf16[3,2,512,128]{2,3,1,0:T(8,128)(2,1)}, bf16[3,2,512,128]{2,3,1,0:T(8,128)(2,1)S(1)}, u32[]{:S(2)}) copy-start(bf16[3,2,512,128]{2,3,1,0:T(8,128)(2,1)S(1)} %fusion.40) | copy-start | bytes 2359300
  418.0 1.1 copy-start.3
  418.1 1.0 copy-start.17
  418.1 1.0 copy-start.37
  420.7 2.8 copy-start.21
  420.7 2.8 copy-start.25
  420.7 2.8 copy-start.35
  555.1 1.5 copy-start.4
  556.7 1.5 copy-start.49
  558.2 1.1 copy-start.10
  558.2 1.4 copy-start.18
Sparse Core Ops, SparseCore 0:
  13.6 22.3 all-gather.22
  38.1 19.6 all-gather.18
  59.9 49.0 all-gather.14
  111.0 47.6 all-gather.20
  273.8 18.1 all-gather.28
  294.0 19.8 all-gather.24
  316.0 49.2 all-gather.26
  367.5 47.6 all-gather.16
